TPU v7x, 128 devices: a whole 4x4x4 slice. The times are simulated.
128 devices in a mesh: seq: 16 (over z, y_lo, core), head: 8 (over x, y_hi).
Axes of the slice: x: 4, y: 4 (y_hi: 2, y_lo: 2; y = y_hi * 2 + y_lo), z: 4, core: 2. Of those that a mesh axis runs over, the one named last changes fastest.
Arguments:
- tokens: bfloat16 [128, 512, 1024], P('seq'), may hold values from -36 to 36
- lengths: int32 [128], P('seq'), may hold values from 1 to 512, 32768 in all
- attn_in: float32 [1024, 3, 1024], P(('seq', 'head')), may hold values from -0.4 to 0.4
- attn_out: float32 [1024, 1024], P(None, ('seq', 'head')), may hold values from -0.1875 to 0.1875
- mlp_in: float32 [1024, 4096], P(('seq', 'head')), may hold values from -0.1875 to 0.1875
- mlp_out: float32 [4096, 1024], P(None, ('seq', 'head')), may hold values from -0.09375 to 0.09375
- norm_gain: float32 [2, 1024], replicated, may hold values from 0.5 to 1.5
- norm_shift: float32 [2, 1024], replicated, may hold values from -3 to 3
Outputs:
- encoded: bfloat16 [128, 512, 1024], P('seq', 'head')
- key_cache: bfloat16 [128, 512, 1024], P('seq', None, 'head')
- value_cache: bfloat16 [128, 512, 1024], P('seq', None, 'head')
Inputs may be any that keep to these rules, and one draw needn't show every extreme that they name: `lengths`: some prompt has exactly 512 tokens.
All inputs are finite; a program needn't handle non-finite values. No bound on the sum of `lengths` on one device may be relied on, other than what follows from the above.
Results may differ from a plain program's by a relative error of at most 0.02.
Values may be sent and summed in bfloat16 or wider, within the bound.
A program may use at most 128 MiB of HBM per device.

v0:
```python
import math
import jax
import jax.numpy as jnp
from jax import lax
from jax.sharding import PartitionSpec as P

DH = 64
EPSILON = 1e-05


def layer_norm(values, gain, shift):
    center = values - jnp.mean(values, axis=-1, keepdims=True)
    spread = jnp.mean(center * center, axis=-1, keepdims=True)
    return center * lax.rsqrt(spread + EPSILON) * gain + shift


def shards(tokens, lengths, attn_in, attn_out, mlp_in, mlp_out, norm_gain, norm_shift):
    heads_axis = lax.axis_size("head")
    head_index = lax.axis_index("head")
    prompts = tokens.shape[0]
    seq_len = tokens.shape[1]
    model_width = tokens.shape[2]
    hidden_width = mlp_in.shape[1]
    block_width = model_width // heads_axis
    hidden_block = hidden_width // heads_axis
    local_heads = block_width // DH
    in_cast = attn_in.astype(jnp.bfloat16)
    up_cast = mlp_in.astype(jnp.bfloat16)
    out_cast = attn_out.astype(jnp.bfloat16)
    down_cast = mlp_out.astype(jnp.bfloat16)
    whole_in, whole_up = (
        lax.all_gather(in_cast, ("seq", "head"), axis=0, tiled=True),
        lax.all_gather(up_cast, ("seq", "head"), axis=0, tiled=True),
    )
    whole_out, whole_down = (
        lax.all_gather(out_cast, ("seq", "head"), axis=1, tiled=True),
        lax.all_gather(down_cast, ("seq", "head"), axis=1, tiled=True),
    )
    qkv_weight = lax.dynamic_slice_in_dim(whole_in, head_index * block_width, block_width, 2)
    up_weight = lax.dynamic_slice_in_dim(whole_up, head_index * hidden_block, hidden_block, 1)
    proj_weight = lax.dynamic_slice_in_dim(whole_out, head_index * block_width, block_width, 0)
    down_weight = lax.dynamic_slice_in_dim(whole_down, head_index * hidden_block, hidden_block, 0)
    projected = jnp.einsum(
        "pld,dte->plte", tokens, qkv_weight, preferred_element_type=jnp.float32
    ).astype(jnp.bfloat16)
    positions = jnp.arange(seq_len, dtype=jnp.int32)
    inside = positions[None, :] < lengths[:, None]
    key_part = projected[:, :, 1]
    value_part = projected[:, :, 2]
    queries = projected[:, :, 0].reshape(prompts, seq_len, local_heads, DH)
    key_heads = key_part.reshape(prompts, seq_len, local_heads, DH)
    value_heads = value_part.reshape(prompts, seq_len, local_heads, DH)
    scores = jnp.einsum(
        "pqhd,pkhd->phqk", queries, key_heads, preferred_element_type=jnp.float32
    ) * (1.0 / math.sqrt(DH))
    scores = jnp.where(inside[:, None, None, :], scores, -1e30)
    row_peak = jnp.max(scores, axis=-1, keepdims=True)
    raised = jnp.exp(scores - row_peak)
    weights = (raised / jnp.sum(raised, axis=-1, keepdims=True)).astype(jnp.bfloat16)
    context = jnp.einsum(
        "phqk,pkhd->pqhd", weights, value_heads, preferred_element_type=jnp.float32
    )
    context = context.astype(jnp.bfloat16).reshape(prompts, seq_len, block_width)
    key_cache = jnp.where(inside[:, :, None], key_part, jnp.zeros_like(key_part))
    value_cache = jnp.where(inside[:, :, None], value_part, jnp.zeros_like(value_part))
    row_count = seq_len // heads_axis
    row_start = head_index * row_count
    attn_partial = jnp.einsum(
        "pld,de->ple", context, proj_weight, preferred_element_type=jnp.float32
    )
    attn_total = lax.psum(attn_partial.astype(jnp.bfloat16), "head").astype(jnp.float32)
    normed = layer_norm(
        tokens.astype(jnp.float32) + attn_total, norm_gain[0], norm_shift[0]
    ).astype(jnp.bfloat16)
    hidden = jax.nn.gelu(
        jnp.einsum("pld,df->plf", normed, up_weight, preferred_element_type=jnp.float32),
        approximate=False,
    ).astype(jnp.bfloat16)
    mlp_partial = jnp.einsum("plf,fe->ple", hidden, down_weight, preferred_element_type=jnp.float32)
    mlp_total = lax.psum(mlp_partial.astype(jnp.bfloat16), "head").astype(jnp.float32)
    mlp_rows = lax.dynamic_slice_in_dim(mlp_total, row_start, row_count, 1)
    normed_rows = lax.dynamic_slice_in_dim(normed, row_start, row_count, 1)
    finished = layer_norm(normed_rows.astype(jnp.float32) + mlp_rows, norm_gain[1], norm_shift[1])
    inside_rows = lax.dynamic_slice_in_dim(inside, row_start, row_count, 1)
    encoded = jnp.where(inside_rows[:, :, None], finished, 0.0).astype(jnp.bfloat16)
    return (encoded, key_cache, value_cache)


def solution(mesh):
    in_specs = (
        P("seq", None, None),
        P("seq"),
        P(("seq", "head"), None, None),
        P(None, ("seq", "head")),
        P(("seq", "head"), None),
        P(None, ("seq", "head")),
        P(),
        P(),
    )
    out_specs = (P("seq", "head", None), P("seq", None, "head"), P("seq", None, "head"))
    return jax.shard_map(shards, mesh=mesh, in_specs=in_specs, out_specs=out_specs, check_vma=False)
```

profile of v0, /device:TPU:5, one launch (start us, length us, event | category | flops | bytes accessed | tf_op | source)
XLA Modules:
  0.0 1998.5 jit_solution(4811427423601753310)
XLA Ops:
  7.2 1.5 convert_element_type.55
  8.8 1.4 convert_element_type.61
  11.0 312.5 %all-gather.5.cloned.1.call-done = bf16[1024,3,1024]{2,0,1:T(8,128)(2,1)} async-done(((bf16[8,3,1024]{2,0,1:T(8,128)(2,1)}), bf16[1024,3,1024]{2,0,1:T(8,128)(2,1)}) %all-gather.5.cloned.1.call-update) | async-done | bytes 6291472 | tf_op jit(solution)/shard_map/all_gather | solution.py:32
  323.5 7.1 convert_bitcast_fusion
  330.6 1.7 fusion.108
  332.4 10.7 fusion.111
  343.1 8.7 fusion.59
  351.8 275.5 %all-gather.7.cloned.1.call-done = bf16[1024,1024]{0,1:T(8,128)(2,1)} async-done(((bf16[1024,8]{0,1:T(8,128)(2,1)}), bf16[1024,1024]{0,1:T(8,128)(2,1)}) %all-gather.7.cloned.1.call-update) | async-done | bytes 2097168 | tf_op jit(solution)/shard_map/all_gather | solution.py:36
  627.3 6.9 convolution_convert_fusion
  636.0 347.3 %all-reduce.3.cloned.1.call-done = bf16[8,512,1024]{2,1,0:T(8,128)(2,1)} async-done(((bf16[8,512,1024]{2,1,0:T(8,128)(2,1)}), bf16[8,512,1024]{2,1,0:T(8,128)(2,1)}) %all-reduce.3.cloned.1.call-update) | async-done | bytes 8388624 | tf_op jit(solution)/shard_map/psum | solution.py:71
  983.3 8.0 fusion.2
  991.3 8.0 multiply_reduce_fusion
  999.7 9.3 add_convert_fusion
  1009.0 286.9 %all-gather.9.cloned.1.call-done = bf16[1024,4096]{1,0:T(8,128)(2,1)} async-done(((bf16[8,4096]{1,0:T(8,128)(2,1)}), bf16[1024,4096]{1,0:T(8,128)(2,1)}) %all-gather.9.cloned.1.call-update) | async-done | bytes 8388624 | tf_op jit(solution)/shard_map/all_gather | solution.py:33
  1295.8 14.5 fusion.54
  1310.3 300.0 %all-gather.11.cloned.1.call-done = bf16[4096,1024]{0,1:T(8,128)(2,1)} async-done(((bf16[4096,8]{0,1:T(8,128)(2,1)}), bf16[4096,1024]{0,1:T(8,128)(2,1)}) %all-gather.11.cloned.1.call-update) | async-done | bytes 8388624 | tf_op jit(solution)/shard_map/all_gather | solution.py:37
  1610.4 25.3 %convolution_convert_fusion.1 = bf16[8,512,1024]{2,1,0:T(8,128)(2,1)} fusion(f32[8,512,512]{2,1,0:T(8,128)} %get-tuple-element.22, u8[512,512]{1,0:T(8,128)(4,1)} %get-tuple-element.10, u8[512,512]{1,0:T(8,128)(4,1)} %get-tuple-element.9, bf16[4096,1024]{0,1:T(8,128)(2,1)} %all-gather.11.cloned.1.call-done, s32[]{:T(128)S(6)} %select_n.31), kind=kOutput, calls=%fused_computation.39 | convolution fusion | flops 4445962240 | bytes 18350084 | tf_op jit(solution)/shard_map/plf,fe->ple/dot_general | solution.py:79
  1635.8 1.5 bitcast_select_fusion
  1637.2 2.3 copy.23
  1639.5 2.3 copy.24
  1641.8 342.7 %all-reduce.5.cloned.1.call-done = bf16[8,512,1024]{2,1,0:T(8,128)(2,1)} async-done(((bf16[8,512,1024]{2,1,0:T(8,128)(2,1)}), bf16[8,512,1024]{2,1,0:T(8,128)(2,1)}) %all-reduce.5.cloned.1.call-update) | async-done | bytes 8388624 | tf_op jit(solution)/shard_map/psum | solution.py:80
  1984.4 1.9 fusion.56
  1986.3 2.0 multiply_reduce_fusion.1
  1988.4 3.2 select_convert_fusion
  (32 shorter events, 3.0 us)
Async XLA Ops:
  7.2 316.3 %all-gather.5.cloned.1.call-start = ((), (), s32[]{:S(2)}) async-start(), calls=%async_computation | async-start | bytes 6340608 | tf_op jit(solution)/shard_map/all_gather | solution.py:32
  8.8 618.6 %all-gather.7.cloned.1.call-start = ((), (), s32[]{:S(2)}) async-start(), calls=%async_computation.1 | async-start | bytes 2113536 | tf_op jit(solution)/shard_map/all_gather | solution.py:36
  10.2 973.1 %all-reduce.3.cloned.1.call-start = ((), (), s32[]{:S(2)}) async-start(), calls=%async_computation.2 | async-start | bytes 16777216 | tf_op jit(solution)/shard_map/psum | solution.py:71
  627.3 7.0 copy-start.1
  627.3 7.7 copy-start.2
  627.3 8.6 copy-start.3
  627.3 8.6 copy-start.4
  634.3 661.5 %all-gather.9.cloned.1.call-start = ((), (), s32[]{:S(2)}) async-start(), calls=%async_computation.3 | async-start | bytes 8454144 | tf_op jit(solution)/shard_map/all_gather | solution.py:33
  635.0 975.4 %all-gather.11.cloned.1.call-start = ((), (), s32[]{:S(2)}) async-start(), calls=%async_computation.4 | async-start | bytes 8454144 | tf_op jit(solution)/shard_map/all_gather | solution.py:37
  635.7 1348.7 %all-reduce.5.cloned.1.call-start = ((), (), s32[]{:S(2)}) async-start(), calls=%async_computation.5 | async-start | bytes 16777216 | tf_op jit(solution)/shard_map/psum | solution.py:80
  991.3 8.4 copy-start
Sparse Core Ops, SparseCore 0:
  10.3 313.1 all-gather.4
  325.2 302.0 all-gather.6
  634.4 348.8 all-reduce.2
  985.4 310.3 all-gather.8
  1297.9 312.4 all-gather.10
  1635.8 348.5 all-reduce.4
where the time goes:
time: 2000 us
  waiting for transfers between devices  1870 us (94%)
  matrix products  73.3 us (4%)
  other arithmetic  38.8 us (2%)
    psum x1, waiting for transfers between devices, shards(): lax.psum(attn_partial.astype(jnp.bfloat16), 'head').astype(jnp.float32)  347 us
    psum x1, waiting for transfers between devices, shards(): lax.psum(mlp_partial.astype(jnp.bfloat16), 'head').astype(jnp.float32)  343 us
    all_gather x1, waiting for transfers between devices, shards(): lax.all_gather(in_cast, ('seq', 'head'), axis=0, tiled=True)  313 us
    all_gather x1, waiting for transfers between devices, shards(): lax.all_gather(down_cast, ('seq', 'head'), axis=1, tiled=True)  300 us
    all_gather x1, waiting for transfers between devices, shards(): lax.all_gather(up_cast, ('seq', 'head'), axis=0, tiled=True)  287 us
    all_gather x1, waiting for transfers between devices, shards(): lax.all_gather(out_cast, ('seq', 'head'), axis=1, tiled=True)  276 us
  transfers between devices with their start and end apart: 6, of which 6 were waited for; matrix products, arithmetic and copies ran while one was open for 4% of the time, Pallas kernels for 0%

commit v1 on v0

--- a/solution.py
+++ b/solution.py
@@ -3,9 +3,11 @@
 import jax.numpy as jnp
 from jax import lax
 from jax.sharding import PartitionSpec as P
+from jax.lax import all_gather
 
 DH = 64
 EPSILON = 1e-05
+_match_lane = lambda here_x, row_axis: jnp.sum(all_gather(here_x, row_axis), axis=0)
 
 
 def layer_norm(values, gain, shift):
@@ -68,7 +70,7 @@
     attn_partial = jnp.einsum(
         "pld,de->ple", context, proj_weight, preferred_element_type=jnp.float32
     )
-    attn_total = lax.psum(attn_partial.astype(jnp.bfloat16), "head").astype(jnp.float32)
+    attn_total = _match_lane(attn_partial.astype(jnp.bfloat16), "head").astype(jnp.float32)
     normed = layer_norm(
         tokens.astype(jnp.float32) + attn_total, norm_gain[0], norm_shift[0]
     ).astype(jnp.bfloat16)

time: 2000 us -> 2300 us (1.15)
  waiting for transfers between devices: 1870 us -> 2140 us
  other arithmetic: 38.8 us -> 64.9 us
    all_gather x0 -> x1, waiting for transfers between devices: none -> 646 us  [all_gather(here_x, row_axis)]
    psum x1 -> x0, waiting for transfers between devices: 347 us -> none  [shards(): lax.psum(attn_partial.astype(jnp.bfloat16), 'head').astype(jnp.float32)]
    reduce_sum x0 -> x1, other arithmetic: none -> 26 us  [jnp.sum(all_gather(here_x, row_axis), axis=0)]
    all_gather x1, waiting for transfers between devices: 287 us -> 262 us  [shards(): lax.all_gather(up_cast, ('seq', 'head'), axis=0, tiled=True)]
  transfers between devices with their start and end apart: 6 -> 6, of which waited for: 6 -> 6; matrix products, arithmetic and copies ran while one was open for 4% -> 5% of each run, Pallas kernels for 0% -> 0%
where the time goes in v1:
time: 2300 us
  waiting for transfers between devices  2140 us (93%)
  matrix products  73.3 us (3%)
  other arithmetic  64.9 us (3%)
    all_gather x1, waiting for transfers between devices, all_gather(here_x, row_axis)  646 us
    psum x1, waiting for transfers between devices, shards(): lax.psum(mlp_partial.astype(jnp.bfloat16), 'head').astype(jnp.float32)  343 us
    all_gather x1, waiting for transfers between devices, shards(): lax.all_gather(in_cast, ('seq', 'head'), axis=0, tiled=True)  313 us
    all_gather x1, waiting for transfers between devices, shards(): lax.all_gather(down_cast, ('seq', 'head'), axis=1, tiled=True)  300 us
    all_gather x1, waiting for transfers between devices, shards(): lax.all_gather(out_cast, ('seq', 'head'), axis=1, tiled=True)  276 us
    all_gather x1, waiting for transfers between devices, shards(): lax.all_gather(up_cast, ('seq', 'head'), axis=0, tiled=True)  262 us
  transfers between devices with their start and end apart: 6, of which 6 were waited for; matrix products, arithmetic and copies ran while one was open for 5% of the time, Pallas kernels for 0%

profile of v1, /device:TPU:5, one launch (start us, length us, event | category | flops | bytes accessed | tf_op | source)
XLA Modules:
  0.0 2298.1 jit_solution(7242184168369301390)
XLA Ops:
  7.2 1.5 convert_element_type.57
  11.0 312.5 %all-gather.7.cloned.1.call-done = bf16[1024,3,1024]{2,0,1:T(8,128)(2,1)} async-done(((bf16[8,3,1024]{2,0,1:T(8,128)(2,1)}), bf16[1024,3,1024]{2,0,1:T(8,128)(2,1)}) %all-gather.7.cloned.1.call-update) | async-done | bytes 6291472 | tf_op jit(solution)/shard_map/all_gather | solution.py:34
  323.5 7.1 convert_bitcast_fusion
  330.6 1.7 fusion.108
  332.4 10.7 fusion.111
  343.1 8.7 fusion.59
  351.8 275.5 %all-gather.9.cloned.1.call-done = bf16[1024,1024]{0,1:T(8,128)(2,1)} async-done(((bf16[1024,8]{0,1:T(8,128)(2,1)}), bf16[1024,1024]{0,1:T(8,128)(2,1)}) %all-gather.9.cloned.1.call-update) | async-done | bytes 2097168 | tf_op jit(solution)/shard_map/all_gather | solution.py:38
  627.3 6.9 convolution_convert_fusion
  636.0 645.8 %all-gather.15.cloned.1.call-done = bf16[64,512,1024]{2,1,0:T(8,128)(2,1)} async-done(((bf16[8,512,1024]{2,1,0:T(8,128)(2,1)}), bf16[64,512,1024]{2,1,0:T(8,128)(2,1)}) %all-gather.15.cloned.1.call-update) | async-done | bytes 67108880 | tf_op jit(solution)/shard_map/all_gather | solution.py:10
  1281.8 26.0 %reduce_sum.58 = bf16[8,512,1024]{2,1,0:T(8,128)(2,1)} reduce(bf16[8,8,512,1024]{3,2,1,0:T(8,128)(2,1)} %bitcast.10, bf16[]{:T(256)} %constant.12.clone.1), dimensions={0}, to_apply=%region_2.3 | reduce | flops 29360128 | bytes 75497472 | tf_op jit(solution)/shard_map/reduce_sum | solution.py:10
  1307.8 8.1 fusion.2
  1315.9 8.1 multiply_reduce_fusion
  1324.2 9.2 add_convert_fusion
  1333.5 262.0 %all-gather.11.cloned.1.call-done = bf16[1024,4096]{1,0:T(8,128)(2,1)} async-done(((bf16[8,4096]{1,0:T(8,128)(2,1)}), bf16[1024,4096]{1,0:T(8,128)(2,1)}) %all-gather.11.cloned.1.call-update) | async-done | bytes 8388624 | tf_op jit(solution)/shard_map/all_gather | solution.py:35
  1595.5 14.5 fusion.54
  1610.0 300.0 %all-gather.13.cloned.1.call-done = bf16[4096,1024]{0,1:T(8,128)(2,1)} async-done(((bf16[4096,8]{0,1:T(8,128)(2,1)}), bf16[4096,1024]{0,1:T(8,128)(2,1)}) %all-gather.13.cloned.1.call-update) | async-done | bytes 8388624 | tf_op jit(solution)/shard_map/all_gather | solution.py:39
  1910.0 25.3 %convolution_convert_fusion.1 = bf16[8,512,1024]{2,1,0:T(8,128)(2,1)} fusion(f32[8,512,512]{2,1,0:T(8,128)} %get-tuple-element.22, u8[512,512]{1,0:T(8,128)(4,1)} %get-tuple-element.10, u8[512,512]{1,0:T(8,128)(4,1)} %get-tuple-element.9, bf16[4096,1024]{0,1:T(8,128)(2,1)} %all-gather.13.cloned.1.call-done, s32[]{:T(128)S(6)} %select_n.31), kind=kOutput, calls=%fused_computation.39 | convolution fusion | flops 4445962240 | bytes 18350084 | tf_op jit(solution)/shard_map/plf,fe->ple/dot_general | solution.py:81
  1935.4 1.5 bitcast_select_fusion
  1936.9 2.3 copy.23
  1939.2 2.3 copy.24
  1941.4 342.7 %all-reduce.2.cloned.1.call-done = bf16[8,512,1024]{2,1,0:T(8,128)(2,1)} async-done(((bf16[8,512,1024]{2,1,0:T(8,128)(2,1)}), bf16[8,512,1024]{2,1,0:T(8,128)(2,1)}) %all-reduce.2.cloned.1.call-update) | async-done | bytes 8388624 | tf_op jit(solution)/shard_map/psum | solution.py:82
  2284.1 1.9 fusion.56
  2286.0 2.0 multiply_reduce_fusion.1
  2288.0 3.2 select_convert_fusion
  (33 shorter events, 4.3 us)
Async XLA Ops:
  7.2 316.3 %all-gather.7.cloned.1.call-start = ((), (), s32[]{:S(2)}) async-start(), calls=%async_computation | async-start | bytes 6340608 | tf_op jit(solution)/shard_map/all_gather | solution.py:34
  8.8 618.6 %all-gather.9.cloned.1.call-start = ((), (), s32[]{:S(2)}) async-start(), calls=%async_computation.1 | async-start | bytes 2113536 | tf_op jit(solution)/shard_map/all_gather | solution.py:38
  10.2 1271.6 %all-gather.15.cloned.1.call-start = ((), (), s32[]{:S(2)}) async-start(), calls=%async_computation.5 | async-start | bytes 75497472 | tf_op jit(solution)/shard_map/all_gather | solution.py:10
  627.3 7.0 copy-start.1
  627.3 7.7 copy-start.2
  627.3 8.6 copy-start.3
  627.3 8.6 copy-start.4
  634.2 961.2 %all-gather.11.cloned.1.call-start = ((), (), s32[]{:S(2)}) async-start(), calls=%async_computation.2 | async-start | bytes 8454144 | tf_op jit(solution)/shard_map/all_gather | solution.py:35
  635.0 1275.1 %all-gather.13.cloned.1.call-start = ((), (), s32[]{:S(2)}) async-start(), calls=%async_computation.3 | async-start | bytes 8454144 | tf_op jit(solution)/shard_map/all_gather | solution.py:39
  635.7 1648.4 %all-reduce.2.cloned.1.call-start = ((), (), s32[]{:S(2)}) async-start(), calls=%async_computation.4 | async-start | bytes 16777216 | tf_op jit(solution)/shard_map/psum | solution.py:82
  1315.9 8.4 copy-start
Sparse Core Ops, SparseCore 0:
  10.3 313.1 all-gather.6
  325.2 302.0 all-gather.8
  634.4 647.3 all-gather.14
  1283.9 311.5 all-gather.10
  1597.6 312.3 all-gather.12
  1935.5 348.5 all-reduce.1
